TPU v7x, 32 devices: a whole 2x2x4 slice. The times are simulated.
32 devices in a mesh: gx: 2 (over y), gy: 4 (over z), gz: 4 (over x, core).
Axes of the slice: x: 2, y: 2, z: 4, core: 2. Of those that a mesh axis runs over, the one named last changes fastest.
Arguments:
- moments: float32 [32, 128, 16, 128], P('gx', ('gy', 'gz')), may hold values from -128 to 128, as said below
- stiffness: float32 [32, 128, 16], P('gx', ('gy', 'gz')), may hold values from 0.5 to 4
- damping: float32 [32, 128, 16], P('gx', ('gy', 'gz')), may hold values from 0.05 to 1
- density: float32 [32, 128, 16], P('gx', ('gy', 'gz')), may hold values from 0.5 to 1.5
- ritz_coeffs: float32 [128, 128], replicated, may hold values from -128 to 128
- shifts: float32 [128], replicated, may hold values from -1.5 to -0.3
Outputs:
- ritz_vectors: float32 [32, 128, 16, 128], P('gx', ('gy', 'gz'))
- ritz_residual: float32 [32, 128, 16, 128], P('gx', ('gy', 'gz'))
- stiff_proj: float32 [128, 128], replicated
- damp_proj: float32 [128, 128], replicated
- mass_proj: float32 [128, 128], replicated
- first_factor: float32 [128, 128], replicated
Inputs may be any that keep to these rules, and one draw needn't show every extreme that they name: `moments`: A real block of full column rank.
All inputs are finite; a program needn't handle non-finite values.
Results may differ from a plain program's by a relative error of at most 0.0004.
Values sent between devices are 32-bit elements; how exact they have to be, the bound alone decides.
A program may use at most 64 MiB of HBM per device.

v0:
```python
import jax
import jax.numpy as jnp
from jax import lax
from jax.sharding import PartitionSpec as P


def with_halo(cells, sides, width):
    for axis, dim in sides:
        count = lax.axis_size(axis)
        ends = count - 1
        head = lax.slice_in_dim(cells, 0, width, axis=dim)
        tail = lax.slice_in_dim(cells, cells.shape[dim] - width, cells.shape[dim], axis=dim)
        cells = jnp.concatenate(
            [
                lax.ppermute(tail, axis, [(i, (i + 1) % count) for i in range(ends)]),
                cells,
                lax.ppermute(head, axis, [((i + 1) % count, i) for i in range(ends)]),
            ],
            axis=dim,
        )
    return cells


def factorize(gram):
    count = gram.shape[0]
    index = jnp.arange(count, dtype=jnp.int32)

    def column_step(j, carry):
        work, lower = carry
        onehot = (index == j).astype(gram.dtype)
        column = jnp.sum(work * onehot[None, :], axis=1)
        pivot = jnp.sum(column * onehot)
        column = jnp.where(index >= j, column, jnp.zeros_like(column)) / jnp.sqrt(pivot)
        lower = lower + column[:, None] * onehot[None, :]
        work = work - column[:, None] * column[None, :]
        return (work, lower)

    start = (gram, jnp.zeros_like(gram))
    lower = lax.fori_loop(0, count, column_step, start)[1]

    def row_step(i, inverse):
        onehot = (index == i).astype(gram.dtype)
        row = jnp.sum(lower * onehot[:, None], axis=0)
        pivot = jnp.sum(row * onehot)
        rhs = onehot - jnp.sum(row[:, None] * inverse, axis=0)
        return inverse + onehot[:, None] * (rhs / pivot)[None, :]

    inverse = lax.fori_loop(0, count, row_step, jnp.zeros_like(gram))
    return (lower, inverse.T)


def matmul(left, right):
    return jnp.dot(left, right, precision=lax.Precision.HIGHEST)


def apply_stencils(flat, shape, stiff_col, dens_col):
    field = flat.reshape(shape)
    padded = with_halo(field, (("gx", 0), (("gy", "gz"), 1)), 1)
    near = padded[2:, 1:-1] + padded[:-2, 1:-1]
    near = near + padded[1:-1, 2:] + padded[1:-1, :-2]
    plane = jnp.zeros((shape[0], shape[1], 1, shape[3]), jnp.float32)
    near = near + jnp.concatenate([field[:, :, 1:], plane], axis=2)
    near = near + jnp.concatenate([plane, field[:, :, :-1]], axis=2)
    near = near.reshape(flat.shape)
    return ((6.0 + stiff_col) * flat - near, dens_col * flat + near / 12.0)


def local(moments, stiffness, damping, density, ritz_coeffs, shifts):
    shape = moments.shape
    cells = shape[0] * shape[1] * shape[2]
    width = shape[3]
    all_cells = cells * lax.axis_size("gx") * lax.axis_size("gy") * lax.axis_size("gz")
    flat = moments.reshape(cells, width)
    stiff_col = stiffness.reshape(cells, 1)
    damp_col = damping.reshape(cells, 1)
    dens_col = density.reshape(cells, 1)
    lower_one, first_inv = factorize(lax.psum(matmul(flat.T, flat), ("gx", "gy", "gz")))
    first_factor = lower_one.T / jnp.sqrt(jnp.float32(all_cells))
    basis_one = matmul(flat, first_inv)
    k_block, m_block = apply_stencils(basis_one, shape, stiff_col, dens_col)
    c_block = damp_col * basis_one
    gram_two, stiff_one, damp_one, mass_one = lax.psum(
        (
            matmul(basis_one.T, basis_one),
            matmul(basis_one.T, k_block),
            matmul(basis_one.T, c_block),
            matmul(basis_one.T, m_block),
        ),
        ("gx", "gy", "gz"),
    )
    second_inv = factorize(gram_two)[1]
    stiff_proj = matmul(second_inv.T, matmul(stiff_one, second_inv))
    damp_proj = matmul(second_inv.T, matmul(damp_one, second_inv))
    mass_proj = matmul(second_inv.T, matmul(mass_one, second_inv))
    coeffs = matmul(second_inv, ritz_coeffs)
    ritz = matmul(basis_one, coeffs)
    resid = matmul(k_block, coeffs)
    resid = resid + matmul(c_block, coeffs) * shifts
    resid = resid + matmul(m_block, coeffs) * (shifts * shifts)
    return (
        ritz.reshape(shape),
        resid.reshape(shape),
        stiff_proj,
        damp_proj,
        mass_proj,
        first_factor,
    )


def solution(mesh):
    return jax.shard_map(
        local,
        mesh=mesh,
        in_specs=(
            P("gx", ("gy", "gz"), None, None),
            P("gx", ("gy", "gz"), None),
            P("gx", ("gy", "gz"), None),
            P("gx", ("gy", "gz"), None),
            P(),
            P(),
        ),
        out_specs=(
            P("gx", ("gy", "gz"), None, None),
            P("gx", ("gy", "gz"), None, None),
            P(),
            P(),
            P(),
            P(),
        ),
        check_vma=False,
    )
```

profile of v0, /device:TPU:0, one launch (start us, length us, event | category | flops | bytes accessed | tf_op | source)
XLA Modules:
  0.0 1594.6 jit_solution(11436615384494239305)
XLA Ops:
  8.4 2.5 convolution_bitcast_fusion
  13.7 120.7 %all-reduce.6.cloned.1.call-done = f32[128,128]{1,0:T(8,128)} async-done(((f32[128,128]{1,0:T(8,128)}), f32[128,128]{1,0:T(8,128)}) %all-reduce.6.cloned.1.call-update) | async-done | bytes 65552 | tf_op jit(solution)/shard_map/psum | solution.py:77
  134.5 488.4 %while.64 = (s32[]{:T(128)}, f32[128,128]{1,0:T(8,128)}, f32[128,128]{1,0:T(8,128)S(1)}, s32[]{:T(128)}, s32[]{:T(128)}) while((s32[]{:T(128)}, f32[128,128]{1,0:T(8,128)}, f32[128,128]{1,0:T(8,128)S(1)}, s32[]{:T(128)}, s32[]{:T(128)}) %tuple.132), condition=%wide.region_4.5_spmd.clone.clone, body=%wide.region_1.4_spmd.clone.clone.sunk | while | flops 115586 | bytes 331875 | solution.py:39
  136.7 1.5 select_add_fusion.4
  144.4 1.5 select_add_fusion.4
  152.0 1.5 select_add_fusion.4
  159.6 1.5 select_add_fusion.4
  163.4 1.5 select_add_fusion.4
  171.1 1.5 select_add_fusion.4
  178.7 1.5 select_add_fusion.4
  186.3 1.5 select_add_fusion.4
  194.0 1.5 select_add_fusion.4
  201.6 1.5 select_add_fusion.4
  209.2 1.5 select_add_fusion.4
  216.9 1.5 select_add_fusion.4
  224.5 1.5 select_add_fusion.4
  622.9 202.8 %while.62 = (s32[]{:T(128)}, f32[128,128]{1,0:T(8,128)S(1)}, f32[128,128]{1,0:T(8,128)S(1)}, s32[]{:T(128)}, s32[]{:T(128)}) while((s32[]{:T(128)}, f32[128,128]{1,0:T(8,128)S(1)}, f32[128,128]{1,0:T(8,128)S(1)}, s32[]{:T(128)}, s32[]{:T(128)}) %tuple.135), condition=%wide.region_9.10_spmd.clone, body=%wide.region_5.9_spmd.clone.sunk | while | flops 131970 | bytes 267356 | solution.py:48
  829.8 4.5 collective-permute-start.1
  834.3 1.6 fusion.39
  835.9 1.7 fusion.21
  839.0 3.9 collective-permute-start.3
  842.9 1.6 fusion.42
  845.8 1.6 copy.18
  847.4 1.7 fusion.28
  849.1 1.7 fusion.26
  851.5 127.3 %all-reduce.8.cloned.1.call-done = (f32[128,128]{1,0:T(8,128)}, f32[128,128]{1,0:T(8,128)}, f32[128,128]{1,0:T(8,128)}, f32[128,128]{1,0:T(8,128)}) async-done(((f32[128,128]{1,0:T(8,128)}, f32[128,128]{1,0:T(8,128)}, f32[128,128]{1,0:T(8,128)}, f32[128,128]{1,0:T(8,128)}), (f32[128,128]{1,0:T(8,128)}, f32[128,128]{1,0:T(8,128)}, f32[128,128]{1,0:T(8,128)}, ...) | async-done | bytes 262160 | tf_op jit(solution)/shard_map/psum | solution.py:82
  978.8 393.4 %while.65 = (s32[]{:T(128)}, f32[128,128]{1,0:T(8,128)}, f32[128,128]{1,0:T(8,128)S(1)}, s32[]{:T(128)}, s32[]{:T(128)}) while((s32[]{:T(128)}, f32[128,128]{1,0:T(8,128)}, f32[128,128]{1,0:T(8,128)S(1)}, s32[]{:T(128)}, s32[]{:T(128)}) %tuple.138), condition=%wide.region_14.15_spmd.clone.clone, body=%wide.region_11.14_spmd.clone.clone.sunk | while | flops 115586 | bytes 856219 | solution.py:39
  1372.2 202.7 %while.63 = (s32[]{:T(128)}, f32[128,128]{1,0:T(8,128)S(1)}, f32[128,128]{1,0:T(8,128)S(1)}, s32[]{:T(128)}, s32[]{:T(128)}) while((s32[]{:T(128)}, f32[128,128]{1,0:T(8,128)S(1)}, f32[128,128]{1,0:T(8,128)S(1)}, s32[]{:T(128)}, s32[]{:T(128)}) %tuple.141), condition=%wide.region_19.0_spmd.clone, body=%wide.region_15.19_spmd.clone.sunk | while | flops 131970 | bytes 267356 | solution.py:48
  1575.2 1.8 fusion.27
  1577.0 2.8 fusion.44
  1583.2 1.8 fusion.15
  1585.0 2.8 fusion.14
  (3378 shorter events, 1085.3 us)
Async XLA Ops:
  7.2 127.3 %all-reduce.6.cloned.1.call-start = ((), (), s32[]{:S(2)}) async-start(), calls=%async_computation | async-start | bytes 131072 | tf_op jit(solution)/shard_map/psum | solution.py:77
  10.9 967.9 %all-reduce.8.cloned.1.call-start = ((), (), s32[]{:S(2)}) async-start(), calls=%async_computation.1 | async-start | bytes 524288 | tf_op jit(solution)/shard_map/psum | solution.py:82
  827.8 9.9 collective-permute-start
  829.8 7.9 collective-permute-start.1
  837.7 6.8 collective-permute-start.2
  839.0 5.5 copy-start.3
  839.0 5.5 copy-start.4
  839.0 5.5 collective-permute-start.3
  984.9 2.3 copy-start.1
  988.0 2.3 copy-start.1
  991.1 2.3 copy-start.1
  1000.3 2.3 copy-start.1
  1003.4 2.3 copy-start.1
  1006.4 2.3 copy-start.1
  1015.7 2.3 copy-start.1
  1018.7 2.3 copy-start.1
  1021.8 2.3 copy-start.1
  1031.0 2.3 copy-start.1
  1034.1 2.3 copy-start.1
  1043.3 2.3 copy-start.1
  1046.4 2.3 copy-start.1
  1049.5 2.3 copy-start.1
  1058.7 2.3 copy-start.1
  1061.8 2.3 copy-start.1
  1064.8 2.3 copy-start.1
  1074.1 2.3 copy-start.1
  1077.1 2.3 copy-start.1
  1080.2 2.3 copy-start.1
  1089.4 2.3 copy-start.1
  1092.5 2.3 copy-start.1
  1372.2 202.7 %copy-start.6 = (f32[128,128]{1,0:T(8,128)S(1)}, f32[128,128]{1,0:T(8,128)}, u32[]{:S(2)}) copy-start(f32[128,128]{1,0:T(8,128)} %param.18) | copy-start | bytes 196612
  1577.0 2.8 copy-start.9
  (244 other events, 338.7 us)
Sparse Core Ops, SparseCore 0:
  14.2 120.2 all-reduce.5
  850.9 127.7 all-reduce.7
where the time goes:
time: 1620 us; the launch traced here: 1590 us
  other arithmetic  1010 us (62%)
  waiting for transfers between devices  248 us (15%)
  loops' own time  197 us (12%)
  local copies, waits for them, and re-layouts  87.3 us (5%)
  matrix products  22.9 us (1%)
    reduce_sum x256, other arithmetic, column_step(): column = jnp.sum(work * onehot[None, :], axis=1)  249 us
    add x256, other arithmetic, column_step(): lower = lower + column[:, None] * onehot[None, :]  209 us
    another operation x2, loops' own time, factorize(): lower = lax.fori_loop(0, count, column_step, start)[1]  186 us
    div x256, other arithmetic, row_step(): return inverse + onehot[:, None] * (rhs / pivot)[None, :]  166 us
    reduce_sum x256, other arithmetic, column_step(): pivot = jnp.sum(column * onehot)  157 us
    reduce_sum x256, other arithmetic, row_step(): pivot = jnp.sum(row * onehot)  155 us
    psum x1, waiting for transfers between devices, local(): lax.psum((matmul(basis_one.T, basis_one), matmul(basis_one.T, k_block), m...  127 us
    psum x1, waiting for transfers between devices, local(): lax.psum(matmul(flat.T, flat), ('gx', 'gy', 'gz'))  121 us
  transfers between devices with their start and end apart: 6, of which 2 were waited for; matrix products, arithmetic and copies ran while one was open for 0% of the time, Pallas kernels for 0%

commit v1 on v0

--- a/solution.py
+++ b/solution.py
@@ -2,6 +2,14 @@
 import jax.numpy as jnp
 from jax import lax
 from jax.sharding import PartitionSpec as P
+
+
+def time_sectors_over_axis(array_here):
+    shard_axis = "gx"
+    axis_key = ("gy", "gz")
+    for t in (axis_key, shard_axis):
+        array_here = lax.psum(array_here, t)
+    return array_here
 
 
 def with_halo(cells, sides, width):
@@ -79,14 +87,13 @@
     basis_one = matmul(flat, first_inv)
     k_block, m_block = apply_stencils(basis_one, shape, stiff_col, dens_col)
     c_block = damp_col * basis_one
-    gram_two, stiff_one, damp_one, mass_one = lax.psum(
+    gram_two, stiff_one, damp_one, mass_one = time_sectors_over_axis(
         (
             matmul(basis_one.T, basis_one),
             matmul(basis_one.T, k_block),
             matmul(basis_one.T, c_block),
             matmul(basis_one.T, m_block),
-        ),
-        ("gx", "gy", "gz"),
+        )
     )
     second_inv = factorize(gram_two)[1]
     stiff_proj = matmul(second_inv.T, matmul(stiff_one, second_inv))

time: 1620 us -> 1510 us (0.932)
  other arithmetic: 1010 us -> 836 us
  local copies, waits for them, and re-layouts: 87.3 us -> 164 us
    add x256, other arithmetic: 209 us -> 23.2 us  [column_step(): lower = lower + column[:, None] * onehot[None, :]]
    while x512 -> x1024, local copies, waits for them, and re-layouts: 78.8 us -> 158 us
    psum x1 -> x2, waiting for transfers between devices: 127 us -> 118 us  [time_sectors_over_axis(): array_here = lax.psum(array_here, t)]
  transfers between devices with their start and end apart: 6 -> 7, of which waited for: 2 -> 4; matrix products, arithmetic and copies ran while one was open for 0% -> 0% of each run, Pallas kernels for 0% -> 0%
where the time goes in v1:
time: 1510 us; the launch traced here: 1490 us
  other arithmetic  836 us (55%)
  waiting for transfers between devices  240 us (16%)
  loops' own time  201 us (13%)
  local copies, waits for them, and re-layouts  164 us (11%)
  matrix products  22.9 us (2%)
    reduce_sum x256, other arithmetic, column_step(): column = jnp.sum(work * onehot[None, :], axis=1)  258 us
    another operation x2, loops' own time, factorize(): lower = lax.fori_loop(0, count, column_step, start)[1]  189 us
    div x256, other arithmetic, row_step(): return inverse + onehot[:, None] * (rhs / pivot)[None, :]  166 us
    while x1024, local copies, waits for them, and re-layouts  158 us
    reduce_sum x256, other arithmetic, column_step(): pivot = jnp.sum(column * onehot)  157 us
    reduce_sum x256, other arithmetic, row_step(): pivot = jnp.sum(row * onehot)  155 us
    psum x1, waiting for transfers between devices, local(): lax.psum(matmul(flat.T, flat), ('gx', 'gy', 'gz'))  122 us
    psum x2, waiting for transfers between devices, time_sectors_over_axis(): array_here = lax.psum(array_here, t)  118 us
  transfers between devices with their start and end apart: 7, of which 4 were waited for; matrix products, arithmetic and copies ran while one was open for 0% of the time, Pallas kernels for 0%

profile of v1, /device:TPU:0, one launch (start us, length us, event | category | flops | bytes accessed | tf_op | source)
XLA Modules:
  0.0 1488.5 jit_solution(18198185822533773569)
XLA Ops:
  7.2 1.2 copy-done
  8.4 2.5 convolution_bitcast_fusion
  12.7 121.8 %all-reduce.8.cloned.1.call-done = f32[128,128]{1,0:T(8,128)} async-done(((f32[128,128]{1,0:T(8,128)}), f32[128,128]{1,0:T(8,128)}) %all-reduce.8.cloned.1.call-update) | async-done | bytes 65552 | tf_op jit(solution)/shard_map/psum | solution.py:85
  134.5 392.6 %while.64 = (s32[]{:T(128)}, f32[128,128]{1,0:T(8,128)}, f32[128,128]{1,0:T(8,128)S(1)}, s32[]{:T(128)}, s32[]{:T(128)}) while((s32[]{:T(128)}, f32[128,128]{1,0:T(8,128)}, f32[128,128]{1,0:T(8,128)S(1)}, s32[]{:T(128)}, s32[]{:T(128)}) %tuple.132), condition=%wide.region_4.5_spmd.clone.clone, body=%wide.region_1.4_spmd.clone.clone.sunk | while | flops 115586 | bytes 856219 | solution.py:47
  527.1 202.8 %while.62 = (s32[]{:T(128)}, f32[128,128]{1,0:T(8,128)S(1)}, f32[128,128]{1,0:T(8,128)S(1)}, s32[]{:T(128)}, s32[]{:T(128)}) while((s32[]{:T(128)}, f32[128,128]{1,0:T(8,128)S(1)}, f32[128,128]{1,0:T(8,128)S(1)}, s32[]{:T(128)}, s32[]{:T(128)}) %tuple.135), condition=%wide.region_9.10_spmd.clone, body=%wide.region_5.9_spmd.clone.sunk | while | flops 131970 | bytes 267356 | solution.py:56
  729.8 1.0 fusion.41
  731.3 1.3 collective-permute-start
  732.7 4.5 collective-permute-start.1
  737.5 1.7 fusion.21
  739.5 1.3 collective-permute-start.2
  740.8 3.3 collective-permute-start.3
  744.1 1.6 fusion.42
  745.7 1.3 fusion.18
  747.0 1.6 copy.18
  748.6 1.7 fusion.28
  750.3 1.7 fusion.26
  752.2 93.0 %all-reduce.10.cloned.1.call-done = (f32[128,128]{1,0:T(8,128)}, f32[128,128]{1,0:T(8,128)}, f32[128,128]{1,0:T(8,128)}, f32[128,128]{1,0:T(8,128)}) async-done(((f32[128,128]{1,0:T(8,128)}, f32[128,128]{1,0:T(8,128)}, f32[128,128]{1,0:T(8,128)}, f32[128,128]{1,0:T(8,128)}), (f32[128,128]{1,0:T(8,128)}, f32[128,128]{1,0:T(8,128)}, f32[128,128]{1,0:T(8,128)}, ...) | async-done | bytes 262160 | tf_op jit(solution)/shard_map/psum | solution.py:11
  846.6 25.1 %all-reduce.12.cloned.1.call-done = (f32[128,128]{1,0:T(8,128)}, f32[128,128]{1,0:T(8,128)}, f32[128,128]{1,0:T(8,128)}, f32[128,128]{1,0:T(8,128)}) async-done(((f32[128,128]{1,0:T(8,128)}, f32[128,128]{1,0:T(8,128)}, f32[128,128]{1,0:T(8,128)}, f32[128,128]{1,0:T(8,128)}), (f32[128,128]{1,0:T(8,128)}, f32[128,128]{1,0:T(8,128)}, f32[128,128]{1,0:T(8,128)}, ...) | async-done | bytes 262160 | tf_op jit(solution)/shard_map/psum | solution.py:11
  871.7 394.6 %while.65 = (s32[]{:T(128)}, f32[128,128]{1,0:T(8,128)}, f32[128,128]{1,0:T(8,128)S(1)}, s32[]{:T(128)}, s32[]{:T(128)}) while((s32[]{:T(128)}, f32[128,128]{1,0:T(8,128)}, f32[128,128]{1,0:T(8,128)S(1)}, s32[]{:T(128)}, s32[]{:T(128)}) %tuple.138), condition=%wide.region_15.16_spmd.clone.clone, body=%wide.region_12.15_spmd.clone.clone.sunk | while | flops 115586 | bytes 856219 | solution.py:47
  874.8 1.0 multiply_reduce_fusion.17
  881.0 1.0 multiply_reduce_fusion.17
  887.2 1.0 multiply_reduce_fusion.17
  896.4 1.0 multiply_reduce_fusion.17
  902.6 1.0 multiply_reduce_fusion.17
  911.8 1.0 multiply_reduce_fusion.17
  918.0 1.0 multiply_reduce_fusion.17
  924.2 1.0 multiply_reduce_fusion.17
  1266.3 202.8 %while.63 = (s32[]{:T(128)}, f32[128,128]{1,0:T(8,128)S(1)}, f32[128,128]{1,0:T(8,128)S(1)}, s32[]{:T(128)}, s32[]{:T(128)}) while((s32[]{:T(128)}, f32[128,128]{1,0:T(8,128)S(1)}, f32[128,128]{1,0:T(8,128)S(1)}, s32[]{:T(128)}, s32[]{:T(128)}) %tuple.141), condition=%wide.region_20.0_spmd.clone, body=%wide.region_16.20_spmd.clone.sunk | while | flops 131970 | bytes 267356 | solution.py:56
  1469.4 1.8 fusion.27
  1471.2 2.8 fusion.44
  1477.3 1.8 fusion.15
  1479.1 2.8 fusion.14
  (3883 shorter events, 992.2 us)
Async XLA Ops:
  7.2 127.3 %all-reduce.8.cloned.1.call-start = ((), (), s32[]{:S(2)}) async-start(), calls=%async_computation | async-start | bytes 131072 | tf_op jit(solution)/shard_map/psum | solution.py:85
  10.9 834.3 %all-reduce.10.cloned.1.call-start = ((), (), s32[]{:S(2)}) async-start(), calls=%async_computation.1 | async-start | bytes 524288 | tf_op jit(solution)/shard_map/psum | solution.py:11
  731.3 7.9 collective-permute-start
  732.7 6.8 collective-permute-start.1
  739.5 6.2 collective-permute-start.2
  740.8 4.9 collective-permute-start.3
  752.0 119.8 %all-reduce.12.cloned.1.call-start = ((), (), s32[]{:S(2)}) async-start(), calls=%async_computation.2 | async-start | bytes 524288 | tf_op jit(solution)/shard_map/psum | solution.py:11
  871.7 2.3 copy-start.1
  874.8 2.3 copy-start.1
  877.9 2.3 copy-start.1
  881.0 2.3 copy-start.1
  884.1 2.3 copy-start.1
  887.2 2.3 copy-start.1
  893.3 2.3 copy-start.1
  896.4 2.3 copy-start.1
  899.5 2.3 copy-start.1
  902.6 2.3 copy-start.1
  905.7 2.3 copy-start.1
  908.7 2.3 copy-start.1
  911.8 2.3 copy-start.1
  914.9 2.3 copy-start.1
  918.0 2.3 copy-start.1
  921.1 2.3 copy-start.1
  924.2 2.3 copy-start.1
  930.3 2.3 copy-start.1
  933.4 2.3 copy-start.1
  936.5 2.3 copy-start.1
  939.6 2.3 copy-start.1
  942.6 2.3 copy-start.1
  945.7 2.3 copy-start.1
  1266.3 202.8 %copy-start.5 = (f32[128,128]{1,0:T(8,128)S(1)}, f32[128,128]{1,0:T(8,128)}, u32[]{:S(2)}) copy-start(f32[128,128]{1,0:T(8,128)} %param.18) | copy-start | bytes 196612
  1471.2 2.8 copy-start.8
  (496 other events, 712.0 us)
Sparse Core Ops, SparseCore 0:
  14.2 120.2 all-reduce.7
  752.1 93.0 all-reduce.9
  847.6 24.0 all-reduce.11

commit v2 on v0

--- a/solution.py
+++ b/solution.py
@@ -2,6 +2,11 @@
 import jax.numpy as jnp
 from jax import lax
 from jax.sharding import PartitionSpec as P
+
+
+def summed_here(x, mesh_axis):
+    pieces = lax.all_gather(x, mesh_axis)
+    return jnp.sum(pieces, axis=0)
 
 
 def with_halo(cells, sides, width):
@@ -74,7 +79,7 @@
     stiff_col = stiffness.reshape(cells, 1)
     damp_col = damping.reshape(cells, 1)
     dens_col = density.reshape(cells, 1)
-    lower_one, first_inv = factorize(lax.psum(matmul(flat.T, flat), ("gx", "gy", "gz")))
+    lower_one, first_inv = factorize(summed_here(matmul(flat.T, flat), ("gx", "gy", "gz")))
     first_factor = lower_one.T / jnp.sqrt(jnp.float32(all_cells))
     basis_one = matmul(flat, first_inv)
     k_block, m_block = apply_stencils(basis_one, shape, stiff_col, dens_col)

time: 1620 us -> 1350 us (0.83)
  other arithmetic: 1010 us -> 901 us
  local copies, waits for them, and re-layouts: 87.3 us -> 7.04 us
  waiting for transfers between devices: 248 us -> 185 us
    psum x1 -> x0, waiting for transfers between devices: 121 us -> none  [local(): lax.psum(matmul(flat.T, flat), ('gx', 'gy', 'gz'))]
    reduce_sum x256, other arithmetic: 249 us -> 134 us  [column_step(): column = jnp.sum(work * onehot[None, :], axis=1)]
    while x512 -> x0, local copies, waits for them, and re-layouts: 78.8 us -> none
    all_gather x0 -> x1, waiting for transfers between devices: none -> 58.3 us  [summed_here(): pieces = lax.all_gather(x, mesh_axis)]
  transfers between devices with their start and end apart: 6 -> 6, of which waited for: 2 -> 2; matrix products, arithmetic and copies ran while one was open for 0% -> 1% of each run, Pallas kernels for 0% -> 0%
where the time goes in v2:
time: 1350 us; the launch traced here: 1340 us
  other arithmetic  901 us (67%)
  loops' own time  197 us (15%)
  waiting for transfers between devices  185 us (14%)
  matrix products  22.9 us (2%)
  between operations  14.4 us (1%)
    add x256, other arithmetic, column_step(): lower = lower + column[:, None] * onehot[None, :]  210 us
    another operation x2, loops' own time, factorize(): lower = lax.fori_loop(0, count, column_step, start)[1]  186 us
    div x256, other arithmetic, row_step(): return inverse + onehot[:, None] * (rhs / pivot)[None, :]  166 us
    reduce_sum x256, other arithmetic, column_step(): pivot = jnp.sum(column * onehot)  157 us
    reduce_sum x256, other arithmetic, row_step(): pivot = jnp.sum(row * onehot)  155 us
    reduce_sum x256, other arithmetic, column_step(): column = jnp.sum(work * onehot[None, :], axis=1)  134 us
    psum x1, waiting for transfers between devices, local(): lax.psum((matmul(basis_one.T, basis_one), matmul(basis_one.T, k_block), m...  127 us
    all_gather x1, waiting for transfers between devices, summed_here(): pieces = lax.all_gather(x, mesh_axis)  58.3 us
  transfers between devices with their start and end apart: 6, of which 2 were waited for; matrix products, arithmetic and copies ran while one was open for 1% of the time, Pallas kernels for 0%

profile of v2, /device:TPU:0, one launch (start us, length us, event | category | flops | bytes accessed | tf_op | source)
XLA Modules:
  0.0 1338.2 jit_solution(5366377119246734215)
XLA Ops:
  8.4 2.5 convolution_bitcast_fusion
  12.4 58.3 %all-gather.3.cloned.1.call-done = f32[4096,128]{1,0:T(8,128)} async-done(((f32[128,128]{1,0:T(8,128)}), f32[4096,128]{1,0:T(8,128)}) %all-gather.3.cloned.1.call-update) | async-done | bytes 2097168 | tf_op jit(solution)/shard_map/all_gather | solution.py:8
  70.7 1.7 reduce_sum.139
  72.4 199.3 %while.64 = (s32[]{:T(128)}, f32[128,128]{1,0:T(8,128)S(1)}, f32[128,128]{1,0:T(8,128)S(1)}, s32[]{:T(128)}, s32[]{:T(128)}) while((s32[]{:T(128)}, f32[128,128]{1,0:T(8,128)S(1)}, f32[128,128]{1,0:T(8,128)S(1)}, s32[]{:T(128)}, s32[]{:T(128)}) %tuple.132), condition=%wide.region_4.5_spmd.clone.clone, body=%wide.region_1.4_spmd.clone.clone.sunk | while | flops 115586 | bytes 331875 | solution.py:44
  271.7 202.8 %while.62 = (s32[]{:T(128)}, f32[128,128]{1,0:T(8,128)S(1)}, f32[128,128]{1,0:T(8,128)S(1)}, s32[]{:T(128)}, s32[]{:T(128)}) while((s32[]{:T(128)}, f32[128,128]{1,0:T(8,128)S(1)}, f32[128,128]{1,0:T(8,128)S(1)}, s32[]{:T(128)}, s32[]{:T(128)}) %tuple.135), condition=%wide.region_9.10_spmd.clone, body=%wide.region_5.9_spmd.clone.sunk | while | flops 131970 | bytes 267356 | solution.py:53
  478.6 4.5 collective-permute-start.1
  483.1 1.6 fusion.39
  484.7 1.7 fusion.21
  487.9 3.2 collective-permute-start.3
  491.2 1.6 fusion.42
  494.1 1.6 copy.18
  495.6 1.7 fusion.28
  497.4 1.7 fusion.26
  499.7 126.9 %all-reduce.5.cloned.1.call-done = (f32[128,128]{1,0:T(8,128)}, f32[128,128]{1,0:T(8,128)}, f32[128,128]{1,0:T(8,128)}, f32[128,128]{1,0:T(8,128)}) async-done(((f32[128,128]{1,0:T(8,128)}, f32[128,128]{1,0:T(8,128)}, f32[128,128]{1,0:T(8,128)}, f32[128,128]{1,0:T(8,128)}), (f32[128,128]{1,0:T(8,128)}, f32[128,128]{1,0:T(8,128)}, f32[128,128]{1,0:T(8,128)}, ...) | async-done | bytes 262160 | tf_op jit(solution)/shard_map/psum | solution.py:87
  626.6 489.2 %while.65 = (s32[]{:T(128)}, f32[128,128]{1,0:T(8,128)}, f32[128,128]{1,0:T(8,128)S(1)}, s32[]{:T(128)}, s32[]{:T(128)}) while((s32[]{:T(128)}, f32[128,128]{1,0:T(8,128)}, f32[128,128]{1,0:T(8,128)S(1)}, s32[]{:T(128)}, s32[]{:T(128)}) %tuple.138), condition=%wide.region_14.15_spmd.clone.clone, body=%wide.region_11.14_spmd.clone.clone.sunk | while | flops 115586 | bytes 331875 | solution.py:44
  628.9 1.6 select_add_fusion.5
  644.2 1.6 select_add_fusion.5
  655.6 1.6 select_add_fusion.5
  659.4 1.6 select_add_fusion.5
  670.9 1.6 select_add_fusion.5
  686.2 1.6 select_add_fusion.5
  701.5 1.6 select_add_fusion.5
  716.8 1.6 select_add_fusion.5
  728.2 1.6 select_add_fusion.5
  732.1 1.6 select_add_fusion.5
  743.5 1.6 select_add_fusion.5
  758.8 1.6 select_add_fusion.5
  1115.8 202.7 %while.63 = (s32[]{:T(128)}, f32[128,128]{1,0:T(8,128)S(1)}, f32[128,128]{1,0:T(8,128)S(1)}, s32[]{:T(128)}, s32[]{:T(128)}) while((s32[]{:T(128)}, f32[128,128]{1,0:T(8,128)S(1)}, f32[128,128]{1,0:T(8,128)S(1)}, s32[]{:T(128)}, s32[]{:T(128)}) %tuple.141), condition=%wide.region_19.0_spmd.clone, body=%wide.region_15.19_spmd.clone.sunk | while | flops 131970 | bytes 267356 | solution.py:53
  1318.9 1.8 fusion.27
  1320.7 2.8 fusion.44
  1326.8 1.8 fusion.15
  1328.6 2.8 fusion.14
  (2867 shorter events, 892.0 us)
Async XLA Ops:
  7.2 1.2 copy-start
  7.2 3.8 copy-start.8
  7.2 3.9 copy-start.10
  7.2 4.6 copy-start.9
  7.2 4.6 copy-start.12
  7.2 63.4 %all-gather.3.cloned.1.call-start = ((), (), s32[]{:S(2)}) async-start(), calls=%async_computation | async-start | bytes 2162688 | tf_op jit(solution)/shard_map/all_gather | solution.py:8
  10.9 615.7 %all-reduce.5.cloned.1.call-start = ((), (), s32[]{:S(2)}) async-start(), calls=%async_computation.1 | async-start | bytes 524288 | tf_op jit(solution)/shard_map/psum | solution.py:87
  476.6 9.9 collective-permute-start
  478.6 7.9 collective-permute-start.1
  486.4 6.4 copy-start.1
  486.4 6.4 copy-start.2
  486.5 6.3 collective-permute-start.2
  487.9 4.9 collective-permute-start.3
  495.6 1.7 copy-start.3
  499.1 819.5 %copy-start.4 = (f32[128,128]{1,0:T(8,128)S(1)}, f32[128,128]{1,0:T(8,128)}, u32[]{:S(2)}) copy-start(f32[128,128]{1,0:T(8,128)} %param.18) | copy-start | bytes 196612
  1318.8 4.6 copy-start.7
  1318.8 5.7 copy-start.6
  1320.7 5.0 copy-start.5
  1320.7 6.1 copy-start.13
  1323.7 4.9 copy-start.11
Sparse Core Ops, SparseCore 0:
  11.5 59.1 all-gather.2
  499.2 127.3 all-reduce.4
